TPU v7x, 32 devices: a whole 2x2x4 slice. The times are simulated.
32 devices in a mesh: tm: 4 (over y, core), expert: 8 (over z, x).
Axes of the slice: x: 2, y: 2, z: 4, core: 2. Of those that a mesh axis runs over, the one named last changes fastest.
Arguments:
- states: bfloat16 [4, 1024, 2048], P('tm', 'expert'), may hold values from -6 to 6
- terminal: float32 [1024, 2048], P('expert'), may hold values from -6 to 6
- gates: float32 [4, 1024, 2], P('tm', 'expert'), may hold values from 0.25 to 1
- routes: int32 [4, 1024, 2], P('tm', 'expert'), may hold values from 0 to 7, all different within a row; in each aligned block of 32 rows (0 to 31, 32 to 63, ..., all dimensions but the last counted through in order) at most 12 rows name the same one
- w_in: bfloat16 [8, 2048, 2048], P('expert'), may hold values from -0.125 to 0.125
- w_out: bfloat16 [8, 2048, 2048], P('expert'), may hold values from -0.125 to 0.125
Outputs:
- adjoints: float32 [4, 1024, 2048], P('tm', 'expert')
Inputs may be any that keep to these rules, and one draw needn't show every extreme that they name: `routes`: the 2 experts of a token at a step differ. In each aligned block of 32 rows of one step (one micro-batch of one device), no expert is named by more than 12 rows, a bound that some block reaches.
All inputs are finite; a program needn't handle non-finite values.
Results may differ from a plain program's by a relative error of at most 0.006.
Values may be sent and summed in bfloat16 or wider, within the bound.
A program may use at most 64 MiB of HBM per device.

v0:
```python
from functools import partial

import jax
import jax.numpy as jnp
from jax import lax
from jax.sharding import PartitionSpec as P

MICRO = 4
MB = 32


step_size = 0.5


def gelu_slope(preact):
    inside = 0.7978845608 * (preact + 0.044715 * preact**3)
    tangent = jnp.tanh(inside)
    return 0.5 * (1.0 + tangent) + 0.5 * preact * (1.0 - tangent * tangent) * 0.7978845608 * (
        1.0 + 3.0 * 0.044715 * preact * preact
    )


def slot_tables(route_rows, expert_count, capacity):
    top_count = route_rows.shape[1]
    flattened = route_rows.reshape(-1)
    onehot = (flattened[:, None] == jnp.arange(expert_count, dtype=jnp.int32)[None, :]).astype(
        jnp.int32
    )
    running = jnp.cumsum(onehot, axis=0)
    slot = jnp.sum(onehot * running, axis=1) - 1
    target = flattened * capacity + slot
    matches = target[None, :] == jnp.arange(expert_count * capacity, dtype=jnp.int32)[:, None]
    filled = jnp.any(matches, axis=1)
    row_ids = jnp.arange(flattened.shape[0], dtype=jnp.int32) // top_count
    source = jnp.sum(matches.astype(jnp.int32) * row_ids[None, :], axis=1)
    return (target, filled, source)


def per_device(states, terminal, gates, routes, w_in, w_out):
    section_count = lax.axis_size("tm")
    section_index = lax.axis_index("tm")
    expert_count = lax.axis_size("expert")
    width = states.shape[2]
    top_count = routes.shape[2]
    micro_count = MICRO
    batch_rows = MB
    capacity = (3 * batch_rows * top_count + 2 * expert_count - 1) // (2 * expert_count)
    weight_in = w_in[0]
    weight_out = w_out[0]
    tables = jax.vmap(partial(slot_tables, expert_count=expert_count, capacity=capacity))

    def pack(rows, filled_row, source_row):
        gathered = jnp.where(filled_row[:, None], rows[source_row], jnp.zeros((), rows.dtype))
        return gathered.reshape(expert_count, capacity, width)

    def backprop(adjoint_rows, slopes):
        back = lax.dot_general(
            adjoint_rows.reshape(-1, width),
            weight_out,
            (((1,), (1,)), ((), ())),
            preferred_element_type=jnp.float32,
        )
        hidden = (back * slopes).astype(jnp.bfloat16)
        return lax.dot_general(
            hidden, weight_in, (((1,), (1,)), ((), ())), preferred_element_type=jnp.float32
        ).astype(jnp.bfloat16)

    def vjp_rows(row_pair):
        state_rows, adjoint_rows = row_pair
        preact = jnp.dot(
            state_rows.reshape(-1, width), weight_in, preferred_element_type=jnp.float32
        )
        return backprop(adjoint_rows, gelu_slope(preact)).reshape(adjoint_rows.shape)

    rows_share = states.shape[1] // section_count
    group_count = max(1, rows_share // batch_rows)
    row_start = section_index * rows_share
    first_block = row_start // batch_rows
    my_states = lax.all_to_all(states, "tm", split_axis=1, concat_axis=0, tiled=True)
    my_gates = lax.all_to_all(gates, "tm", split_axis=1, concat_axis=0, tiled=True)
    every_route = lax.all_gather(routes, "tm", axis=0, tiled=True)
    my_terminal = lax.dynamic_slice_in_dim(terminal, row_start, rows_share, 0)
    block_ids = first_block + jnp.arange(group_count, dtype=jnp.int32)
    row_blocks = (row_start + jnp.arange(rows_share, dtype=jnp.int32)) // batch_rows - first_block
    pack_many = jax.vmap(pack, in_axes=(None, 0, 0))

    def one_round(turn, carry):
        adjoint, collected = carry
        step = section_count - 1 - turn
        step_routes = lax.dynamic_index_in_dim(every_route, step, 0, keepdims=False)
        block_routes = lax.dynamic_slice_in_dim(
            step_routes.reshape(micro_count, batch_rows, top_count), first_block, group_count, 0
        )
        targets, filled_all, sources = tables(block_routes)
        local_source = sources + block_ids[:, None] * batch_rows - row_start
        mine = jnp.logical_and(
            filled_all, jnp.logical_and(local_source >= 0, local_source < rows_share)
        )
        clipped = jnp.clip(local_source, 0, rows_share - 1)
        state_rows = lax.dynamic_index_in_dim(my_states, step, 0, keepdims=False)
        state_send = pack_many(state_rows, mine, clipped)
        adjoint_send = pack_many(adjoint.astype(jnp.bfloat16), mine, clipped)
        answers = vjp_rows(
            (
                lax.all_to_all(state_send, "expert", split_axis=1, concat_axis=1, tiled=True),
                lax.all_to_all(adjoint_send, "expert", split_axis=1, concat_axis=1, tiled=True),
            )
        )
        returned = lax.all_to_all(answers, "expert", split_axis=1, concat_axis=1, tiled=True)
        target_rows = targets.reshape(group_count * batch_rows, top_count)
        my_targets = lax.dynamic_slice_in_dim(
            target_rows, row_start - first_block * batch_rows, rows_share, 0
        )
        my_targets = my_targets + row_blocks[:, None] * (expert_count * capacity)
        picked = returned.reshape(-1, width)[my_targets].astype(jnp.float32)
        step_gates = lax.dynamic_index_in_dim(my_gates, step, 0, keepdims=False)
        combined = jnp.sum(step_gates[:, :, None] * picked, axis=1)
        updated = adjoint + step_size * combined
        collected = lax.dynamic_update_index_in_dim(collected, updated, step, 0)
        return (updated, collected)

    initial = (my_terminal, jnp.zeros((section_count, rows_share, width), jnp.float32))
    _, collected = lax.fori_loop(0, section_count, one_round, initial)
    return lax.all_to_all(collected, "tm", split_axis=0, concat_axis=1, tiled=True)


def solution(mesh):
    placed = (
        P("tm", "expert", None),
        P("expert", None),
        P("tm", "expert", None),
        P("tm", "expert", None),
        P("expert", None, None),
        P("expert", None, None),
    )
    return jax.shard_map(
        per_device, mesh=mesh, in_specs=placed, out_specs=P("tm", "expert", None), check_vma=False
    )
```

profile of v0, /device:TPU:0, one launch (start us, length us, event | category | flops | bytes accessed | tf_op | source)
XLA Modules:
  0.0 341.4 jit_solution(2866869326601038428)
XLA Ops:
  1.5 4.3 %all-to-all-start.3 = ((f32[1,128,2]{2,0,1:T(1,128)}), f32[1,128,2]{2,0,1:T(1,128)S(1)}, u32[]{:S(2)}, u32[]{:S(2)}) async-start(f32[1,128,2]{2,0,1:T(1,128)} %copy.45), calls=%async_computation.3 | async-start | bytes 131072 | tf_op jit(solution)/shard_map/all_to_all | solution.py:80
  16.5 9.6 %all_gather.3 = s32[4,128,2]{1,2,0:T(2,128)S(1)} all-gather(s32[1,128,2]{1,2,0:T(2,128)} %param.11), channel_id=1, replica_groups=mesh['tm'=4,'expert'=8] {'tm'}, dimensions={0}, use_global_device_ids=true | all-gather | bytes 5120 | tf_op jit(solution)/shard_map/all_gather | solution.py:81
  28.2 294.3 %while.20 = (s32[]{:T(128)}, f32[32,2048]{1,0:T(8,128)S(1)}, f32[4,32,2048]{2,1,0:T(8,128)}, f32[4,32,2]{1,2,0:T(2,128)S(1)}, s32[4,128,2]{1,2,0:T(2,128)S(1)}, ...) while((s32[]{:T(128)}, f32[32,2048]{1,0:T(8,128)S(1)}, ...), condition=%wide.region_6.7_spmd.clone.clone, body=%wide.region_0.6_spmd.clone.clone.sunk | while | flops 2420707584 | bytes 43287280 | solution.py:123
  32.1 21.1 %all_to_all.85 = bf16[1,8,12,2048]{3,2,0,1:T(8,128)(2,1)S(1)} all-to-all(bf16[1,8,12,2048]{3,2,0,1:T(8,128)(2,1)S(1)} %get-tuple-element.546), channel_id=1, replica_groups=mesh['tm'=4,'expert'=8] {'expert'}, dimensions={1} | all-to-all | bytes 786432 | tf_op jit(solution)/shard_map/while/body/eval_jaxpr/all_to_all | solution.py:105
  56.9 4.8 %fusion.48 = f32[96,2048]{1,0:T(8,128)S(1)} fusion(bf16[96,2048]{1,0:T(8,128)(2,1)S(1)} %reshape.642, bf16[2048,2048]{1,0:T(8,128)(2,1)} %get-tuple-element.593), kind=kOutput, calls=%fused_computation.63.clone.1 | convolution fusion | flops 805306368 | bytes 9568256 | tf_op jit(solution)/shard_map/while/body/eval_jaxpr/dot_general | solution.py:70
  61.7 9.6 %all-to-all-done = bf16[1,8,12,2048]{3,2,0,1:T(8,128)(2,1)S(1)} async-done(((bf16[1,8,12,2048]{3,2,0,1:T(8,128)(2,1)}), bf16[1,8,12,2048]{3,2,0,1:T(8,128)(2,1)S(1)}, u32[]{:S(2)}, u32[]{:S(2)}) %all-to-all-start) | async-done | bytes 393248 | tf_op jit(solution)/shard_map/while/body/eval_jaxpr/all_to_all | solution.py:106
  71.5 11.1 %convolution_convert_fusion.2 = bf16[96,2048]{1,0:T(8,128)(2,1)S(1)} fusion(bf16[2048,2048]{1,0:T(8,128)(2,1)} %get-tuple-element.593, bf16[96,2048]{1,0:T(8,128)(2,1)S(1)} %reshape.641, bf16[2048,2048]{1,0:T(8,128)(2,1)} %get-tuple-element.591, f32[96,2048]{1,0:T(8,128)S(1)} %fusion.48), kind=kOutput, calls=%fused_computation.6.clone.1 | convolution fusion | flops 1614544896 | bytes 18350080 | tf_op jit(solution)/shard_map/while/body/eval_jaxpr/dot_general | solution.py:64
  87.6 14.1 %all-to-all-done.2 = bf16[1,8,12,2048]{3,2,0,1:T(8,128)(2,1)S(1)} async-done(((bf16[1,8,12,2048]{3,2,0,1:T(8,128)(2,1)}), bf16[1,8,12,2048]{3,2,0,1:T(8,128)(2,1)S(1)}, u32[]{:S(2)}, u32[]{:S(2)}) %all-to-all-start.2) | async-done | bytes 393248 | tf_op jit(solution)/shard_map/while/body/eval_jaxpr/all_to_all | solution.py:109
  108.4 18.1 %all_to_all.85 = bf16[1,8,12,2048]{3,2,0,1:T(8,128)(2,1)S(1)} all-to-all(bf16[1,8,12,2048]{3,2,0,1:T(8,128)(2,1)S(1)} %get-tuple-element.546), channel_id=1, replica_groups=mesh['tm'=4,'expert'=8] {'expert'}, dimensions={1} | all-to-all | bytes 786432 | tf_op jit(solution)/shard_map/while/body/eval_jaxpr/all_to_all | solution.py:105
  130.2 4.8 %fusion.48 = f32[96,2048]{1,0:T(8,128)S(1)} fusion(bf16[96,2048]{1,0:T(8,128)(2,1)S(1)} %reshape.642, bf16[2048,2048]{1,0:T(8,128)(2,1)} %get-tuple-element.593), kind=kOutput, calls=%fused_computation.63.clone.1 | convolution fusion | flops 805306368 | bytes 9568256 | tf_op jit(solution)/shard_map/while/body/eval_jaxpr/dot_general | solution.py:70
  135.0 9.2 %all-to-all-done = bf16[1,8,12,2048]{3,2,0,1:T(8,128)(2,1)S(1)} async-done(((bf16[1,8,12,2048]{3,2,0,1:T(8,128)(2,1)}), bf16[1,8,12,2048]{3,2,0,1:T(8,128)(2,1)S(1)}, u32[]{:S(2)}, u32[]{:S(2)}) %all-to-all-start) | async-done | bytes 393248 | tf_op jit(solution)/shard_map/while/body/eval_jaxpr/all_to_all | solution.py:106
  144.4 11.1 %convolution_convert_fusion.2 = bf16[96,2048]{1,0:T(8,128)(2,1)S(1)} fusion(bf16[2048,2048]{1,0:T(8,128)(2,1)} %get-tuple-element.593, bf16[96,2048]{1,0:T(8,128)(2,1)S(1)} %reshape.641, bf16[2048,2048]{1,0:T(8,128)(2,1)} %get-tuple-element.591, f32[96,2048]{1,0:T(8,128)S(1)} %fusion.48), kind=kOutput, calls=%fused_computation.6.clone.1 | convolution fusion | flops 1614544896 | bytes 18350080 | tf_op jit(solution)/shard_map/while/body/eval_jaxpr/dot_general | solution.py:64
  160.5 13.9 %all-to-all-done.2 = bf16[1,8,12,2048]{3,2,0,1:T(8,128)(2,1)S(1)} async-done(((bf16[1,8,12,2048]{3,2,0,1:T(8,128)(2,1)}), bf16[1,8,12,2048]{3,2,0,1:T(8,128)(2,1)S(1)}, u32[]{:S(2)}, u32[]{:S(2)}) %all-to-all-start.2) | async-done | bytes 393248 | tf_op jit(solution)/shard_map/while/body/eval_jaxpr/all_to_all | solution.py:109
  181.0 18.1 %all_to_all.85 = bf16[1,8,12,2048]{3,2,0,1:T(8,128)(2,1)S(1)} all-to-all(bf16[1,8,12,2048]{3,2,0,1:T(8,128)(2,1)S(1)} %get-tuple-element.546), channel_id=1, replica_groups=mesh['tm'=4,'expert'=8] {'expert'}, dimensions={1} | all-to-all | bytes 786432 | tf_op jit(solution)/shard_map/while/body/eval_jaxpr/all_to_all | solution.py:105
  202.8 4.8 %fusion.48 = f32[96,2048]{1,0:T(8,128)S(1)} fusion(bf16[96,2048]{1,0:T(8,128)(2,1)S(1)} %reshape.642, bf16[2048,2048]{1,0:T(8,128)(2,1)} %get-tuple-element.593), kind=kOutput, calls=%fused_computation.63.clone.1 | convolution fusion | flops 805306368 | bytes 9568256 | tf_op jit(solution)/shard_map/while/body/eval_jaxpr/dot_general | solution.py:70
  207.7 9.2 %all-to-all-done = bf16[1,8,12,2048]{3,2,0,1:T(8,128)(2,1)S(1)} async-done(((bf16[1,8,12,2048]{3,2,0,1:T(8,128)(2,1)}), bf16[1,8,12,2048]{3,2,0,1:T(8,128)(2,1)S(1)}, u32[]{:S(2)}, u32[]{:S(2)}) %all-to-all-start) | async-done | bytes 393248 | tf_op jit(solution)/shard_map/while/body/eval_jaxpr/all_to_all | solution.py:106
  217.0 11.1 %convolution_convert_fusion.2 = bf16[96,2048]{1,0:T(8,128)(2,1)S(1)} fusion(bf16[2048,2048]{1,0:T(8,128)(2,1)} %get-tuple-element.593, bf16[96,2048]{1,0:T(8,128)(2,1)S(1)} %reshape.641, bf16[2048,2048]{1,0:T(8,128)(2,1)} %get-tuple-element.591, f32[96,2048]{1,0:T(8,128)S(1)} %fusion.48), kind=kOutput, calls=%fused_computation.6.clone.1 | convolution fusion | flops 1614544896 | bytes 18350080 | tf_op jit(solution)/shard_map/while/body/eval_jaxpr/dot_general | solution.py:64
  233.2 13.9 %all-to-all-done.2 = bf16[1,8,12,2048]{3,2,0,1:T(8,128)(2,1)S(1)} async-done(((bf16[1,8,12,2048]{3,2,0,1:T(8,128)(2,1)}), bf16[1,8,12,2048]{3,2,0,1:T(8,128)(2,1)S(1)}, u32[]{:S(2)}, u32[]{:S(2)}) %all-to-all-start.2) | async-done | bytes 393248 | tf_op jit(solution)/shard_map/while/body/eval_jaxpr/all_to_all | solution.py:109
  253.7 18.1 %all_to_all.85 = bf16[1,8,12,2048]{3,2,0,1:T(8,128)(2,1)S(1)} all-to-all(bf16[1,8,12,2048]{3,2,0,1:T(8,128)(2,1)S(1)} %get-tuple-element.546), channel_id=1, replica_groups=mesh['tm'=4,'expert'=8] {'expert'}, dimensions={1} | all-to-all | bytes 786432 | tf_op jit(solution)/shard_map/while/body/eval_jaxpr/all_to_all | solution.py:105
  275.5 4.8 %fusion.48 = f32[96,2048]{1,0:T(8,128)S(1)} fusion(bf16[96,2048]{1,0:T(8,128)(2,1)S(1)} %reshape.642, bf16[2048,2048]{1,0:T(8,128)(2,1)} %get-tuple-element.593), kind=kOutput, calls=%fused_computation.63.clone.1 | convolution fusion | flops 805306368 | bytes 9568256 | tf_op jit(solution)/shard_map/while/body/eval_jaxpr/dot_general | solution.py:70
  280.3 9.2 %all-to-all-done = bf16[1,8,12,2048]{3,2,0,1:T(8,128)(2,1)S(1)} async-done(((bf16[1,8,12,2048]{3,2,0,1:T(8,128)(2,1)}), bf16[1,8,12,2048]{3,2,0,1:T(8,128)(2,1)S(1)}, u32[]{:S(2)}, u32[]{:S(2)}) %all-to-all-start) | async-done | bytes 393248 | tf_op jit(solution)/shard_map/while/body/eval_jaxpr/all_to_all | solution.py:106
  289.7 11.1 %convolution_convert_fusion.2 = bf16[96,2048]{1,0:T(8,128)(2,1)S(1)} fusion(bf16[2048,2048]{1,0:T(8,128)(2,1)} %get-tuple-element.593, bf16[96,2048]{1,0:T(8,128)(2,1)S(1)} %reshape.641, bf16[2048,2048]{1,0:T(8,128)(2,1)} %get-tuple-element.591, f32[96,2048]{1,0:T(8,128)S(1)} %fusion.48), kind=kOutput, calls=%fused_computation.6.clone.1 | convolution fusion | flops 1614544896 | bytes 18350080 | tf_op jit(solution)/shard_map/while/body/eval_jaxpr/dot_general | solution.py:64
  305.9 13.9 %all-to-all-done.2 = bf16[1,8,12,2048]{3,2,0,1:T(8,128)(2,1)S(1)} async-done(((bf16[1,8,12,2048]{3,2,0,1:T(8,128)(2,1)}), bf16[1,8,12,2048]{3,2,0,1:T(8,128)(2,1)S(1)}, u32[]{:S(2)}, u32[]{:S(2)}) %all-to-all-start.2) | async-done | bytes 393248 | tf_op jit(solution)/shard_map/while/body/eval_jaxpr/all_to_all | solution.py:109
  322.5 17.9 %all_to_all.84 = f32[4,32,2048]{2,1,0:T(8,128)S(1)} all-to-all(f32[4,32,2048]{2,1,0:T(8,128)} %get-tuple-element.320), channel_id=1, replica_groups=mesh['tm'=4,'expert'=8] {'tm'}, dimensions={0} | all-to-all | bytes 2097152 | tf_op jit(solution)/shard_map/all_to_all | solution.py:124
  (180 shorter events, 76.4 us)
Async XLA Ops:
  0.0 26.2 %copy-start = (f32[128,2048]{1,0:T(8,128)S(1)}, f32[128,2048]{1,0:T(8,128)}, u32[]{:S(2)}) copy-start(f32[128,2048]{1,0:T(8,128)} %param.9) | copy-start | bytes 3145732
  1.5 11.5 %all-to-all-start.3 = ((f32[1,128,2]{2,0,1:T(1,128)}), f32[1,128,2]{2,0,1:T(1,128)S(1)}, u32[]{:S(2)}, u32[]{:S(2)}) async-start(f32[1,128,2]{2,0,1:T(1,128)} %copy.45), calls=%async_computation.3 | async-start | bytes 131072 | tf_op jit(solution)/shard_map/all_to_all | solution.py:80
  13.0 13.3 %all-to-all-start.4 = ((bf16[4,2,32768]{2,1,0:T(2,128)(2,1)}), bf16[4,2,32768]{2,1,0:T(2,128)(2,1)S(1)}, u32[]{:S(2)}, u32[]{:S(2)}) async-start(bf16[4,2,32768]{2,1,0:T(2,128)(2,1)} %reshape.615), calls=%async_computation.4 | async-start | bytes 1048576 | tf_op jit(solution)/shard_map/all_to_all | solution.py:79
  53.2 18.2 %all-to-all-start = ((bf16[1,8,12,2048]{3,2,0,1:T(8,128)(2,1)}), bf16[1,8,12,2048]{3,2,0,1:T(8,128)(2,1)S(1)}, u32[]{:S(2)}, u32[]{:S(2)}) async-start(bf16[1,8,12,2048]{3,2,0,1:T(8,128)(2,1)} %get-tuple-element.545), calls=%async_computation | async-start | bytes 1048576 | tf_op jit(solution)/shard_map/while/body/eval_jaxpr/all_to_all | solution.py:106
  83.5 18.3 %all-to-all-start.2 = ((bf16[1,8,12,2048]{3,2,0,1:T(8,128)(2,1)}), bf16[1,8,12,2048]{3,2,0,1:T(8,128)(2,1)S(1)}, u32[]{:S(2)}, u32[]{:S(2)}) async-start(bf16[1,8,12,2048]{3,2,0,1:T(8,128)(2,1)} %bitcast.68), calls=%async_computation.2 | async-start | bytes 1048576 | tf_op jit(solution)/shard_map/while/body/eval_jaxpr/all_to_all | solution.py:109
  126.5 17.8 %all-to-all-start = ((bf16[1,8,12,2048]{3,2,0,1:T(8,128)(2,1)}), bf16[1,8,12,2048]{3,2,0,1:T(8,128)(2,1)S(1)}, u32[]{:S(2)}, u32[]{:S(2)}) async-start(bf16[1,8,12,2048]{3,2,0,1:T(8,128)(2,1)} %get-tuple-element.545), calls=%async_computation | async-start | bytes 1048576 | tf_op jit(solution)/shard_map/while/body/eval_jaxpr/all_to_all | solution.py:106
  156.4 18.1 %all-to-all-start.2 = ((bf16[1,8,12,2048]{3,2,0,1:T(8,128)(2,1)}), bf16[1,8,12,2048]{3,2,0,1:T(8,128)(2,1)S(1)}, u32[]{:S(2)}, u32[]{:S(2)}) async-start(bf16[1,8,12,2048]{3,2,0,1:T(8,128)(2,1)} %bitcast.68), calls=%async_computation.2 | async-start | bytes 1048576 | tf_op jit(solution)/shard_map/while/body/eval_jaxpr/all_to_all | solution.py:109
  199.1 17.8 %all-to-all-start = ((bf16[1,8,12,2048]{3,2,0,1:T(8,128)(2,1)}), bf16[1,8,12,2048]{3,2,0,1:T(8,128)(2,1)S(1)}, u32[]{:S(2)}, u32[]{:S(2)}) async-start(bf16[1,8,12,2048]{3,2,0,1:T(8,128)(2,1)} %get-tuple-element.545), calls=%async_computation | async-start | bytes 1048576 | tf_op jit(solution)/shard_map/while/body/eval_jaxpr/all_to_all | solution.py:106
  229.0 18.1 %all-to-all-start.2 = ((bf16[1,8,12,2048]{3,2,0,1:T(8,128)(2,1)}), bf16[1,8,12,2048]{3,2,0,1:T(8,128)(2,1)S(1)}, u32[]{:S(2)}, u32[]{:S(2)}) async-start(bf16[1,8,12,2048]{3,2,0,1:T(8,128)(2,1)} %bitcast.68), calls=%async_computation.2 | async-start | bytes 1048576 | tf_op jit(solution)/shard_map/while/body/eval_jaxpr/all_to_all | solution.py:109
  271.8 17.8 %all-to-all-start = ((bf16[1,8,12,2048]{3,2,0,1:T(8,128)(2,1)}), bf16[1,8,12,2048]{3,2,0,1:T(8,128)(2,1)S(1)}, u32[]{:S(2)}, u32[]{:S(2)}) async-start(bf16[1,8,12,2048]{3,2,0,1:T(8,128)(2,1)} %get-tuple-element.545), calls=%async_computation | async-start | bytes 1048576 | tf_op jit(solution)/shard_map/while/body/eval_jaxpr/all_to_all | solution.py:106
  301.7 18.1 %all-to-all-start.2 = ((bf16[1,8,12,2048]{3,2,0,1:T(8,128)(2,1)}), bf16[1,8,12,2048]{3,2,0,1:T(8,128)(2,1)S(1)}, u32[]{:S(2)}, u32[]{:S(2)}) async-start(bf16[1,8,12,2048]{3,2,0,1:T(8,128)(2,1)} %bitcast.68), calls=%async_computation.2 | async-start | bytes 1048576 | tf_op jit(solution)/shard_map/while/body/eval_jaxpr/all_to_all | solution.py:109
where the time goes:
time: 343 us; the launch traced here: 341 us
  blocking collectives  103 us (30%)
  waiting for transfers between devices  93.2 us (27%)
  matrix products  63.9 us (19%)
  starting transfers between devices  36.8 us (11%)
  local copies, waits for them, and re-layouts  27.7 us (8%)
  other arithmetic  16.1 us (5%)
    all_to_all x4, blocking collectives, one_round(): lax.all_to_all(state_send, 'expert', split_axis=1, concat_axis=1, tiled=T...  75.4 us
    all_to_all x4, waiting for transfers between devices, one_round(): lax.all_to_all(answers, 'expert', split_axis=1, concat_axis=1, tiled=True)  55.9 us
    dot_general x4, matrix products, backprop(): lax.dot_general(hidden, weight_in, (((1,), (1,)), ((), ())), preferred_el...  44.5 us
    all_to_all x4, waiting for transfers between devices, one_round(): lax.all_to_all(adjoint_send, 'expert', split_axis=1, concat_axis=1, tiled...  37.4 us
    dot_general x4, matrix products, vjp_rows(): jnp.dot(state_rows.reshape(-1, width), weight_in, preferred_element_type=...  19.3 us
    all_to_all x1, blocking collectives, per_device(): lax.all_to_all(collected, 'tm', split_axis=0, concat_axis=1, tiled=True)  17.9 us
    all_to_all x4, starting transfers between devices, one_round(): lax.all_to_all(adjoint_send, 'expert', split_axis=1, concat_axis=1, tiled...  14.5 us
    all_to_all x4, starting transfers between devices, one_round(): lax.all_to_all(answers, 'expert', split_axis=1, concat_axis=1, tiled=True)  14.5 us
  transfers between devices with their start and end apart: 10, of which 8 were waited for; matrix products, arithmetic and copies ran while one was open for 8% of the time, Pallas kernels for 0%

commit v1 on v0

v1 whole, which is shorter than its diff:
```python
import functools

import jax
import jax.numpy as jnp
from jax import lax
from jax.experimental import pallas as pl
from jax.experimental.pallas import tpu as pltpu
from jax.sharding import PartitionSpec as P

MB = 32
CHUNKS = 4
STEP_SIZE = 0.5
PAD = 16


def gelu_slope(v):
    inside = 0.7978845608 * (v + 0.044715 * (v * v * v))
    t = jnp.tanh(inside)
    return 0.5 * (1.0 + t) + 0.5 * v * (1.0 - t * t) * 0.7978845608 * (
        1.0 + 3.0 * 0.044715 * v * v
    )


def kernel(
    steps, experts, cap, rows,
    states, terminal, rg, w_in, w_out,
    out,
    win, wout, adj, sts, rgb, pmat, cmat, send_s, recv_s, send_a, recv_a, send_b, recv_b,
    slopes, back, hidden, collect,
    w_sem, loc_sem, rg_ssem, rg_rsem, st_ssem, st_rsem,
    s_ssem, s_rsem, a_ssem, a_rsem, b_ssem, b_rsem, o_ssem, o_rsem,
):
    t = lax.axis_index("tm")
    me = lax.axis_index("expert")
    width = win.shape[0]
    ff = win.shape[1]
    dc = width // CHUNKS
    fc = ff // CHUNKS
    slots = experts * PAD

    def cols(c):
        return pl.ds(c * dc, dc)

    def slab(e):
        return pl.ds(pl.multiple_of(e * PAD, PAD), PAD)

    def peer(k):
        return lax.rem(me + k, experts)

    def tm_peer(k):
        return lax.rem(t + k, steps)

    def remote(src, dst, ssem, rsem, axis, dev):
        return pltpu.make_async_remote_copy(
            src_ref=src, dst_ref=dst, send_sem=ssem, recv_sem=rsem,
            device_id={axis: dev}, device_id_type=pl.DeviceIdType.MESH,
        )

    def block_rows(b):
        return pl.ds(pl.multiple_of(b * rows, rows), rows)

    def w_copies():
        found = []
        for c in range(CHUNKS):
            part = pl.ds(c * fc, fc)
            found.append(pltpu.make_async_copy(w_in.at[0, :, part], win.at[:, part], w_sem.at[0, c]))
        for c in range(CHUNKS):
            found.append(
                pltpu.make_async_copy(w_out.at[0, :, cols(c)], wout.at[:, cols(c)], w_sem.at[1, c])
            )
        return found

    own_terminal = pltpu.make_async_copy(terminal.at[block_rows(t)], adj, loc_sem.at[0])
    own_terminal.start()
    own_states = pltpu.make_async_copy(states.at[0, block_rows(t)], sts.at[t], loc_sem.at[1])
    own_states.start()
    own_rg = pltpu.make_async_copy(rg.at[block_rows(t)], rgb.at[t], loc_sem.at[2])
    own_rg.start()
    weights = w_copies()
    for copy in weights:
        copy.start()

    zeros = jnp.zeros((slots, width), jnp.bfloat16)
    recv_a[...] = zeros
    recv_b[...] = zeros
    for s in range(steps):
        recv_s[s] = zeros

    barrier = pltpu.get_barrier_semaphore()
    for k in range(1, experts):
        pl.semaphore_signal(
            barrier, inc=1, device_id={"expert": peer(k)}, device_id_type=pl.DeviceIdType.MESH
        )
    for k in range(1, steps):
        pl.semaphore_signal(
            barrier, inc=1, device_id={"tm": tm_peer(k)}, device_id_type=pl.DeviceIdType.MESH
        )
    pl.semaphore_wait(barrier, experts + steps - 2)

    def rg_copy(k):
        b = tm_peer(k)
        return remote(rg.at[block_rows(b)], rgb.at[t], rg_ssem.at[k - 1], rg_rsem.at[k - 1], "tm", b)

    def st_copy(k):
        b = tm_peer(k)
        return remote(
            states.at[0, block_rows(b)], sts.at[t], st_ssem.at[k - 1], st_rsem.at[k - 1], "tm", b
        )

    for k in range(1, steps):
        rg_copy(k).start()
    for k in range(1, steps):
        st_copy(k).start()

    own_rg.wait()
    for k in range(1, steps):
        rg_copy(k).wait()

    lane = lax.broadcasted_iota(jnp.int32, (rows, slots), 1)
    lane_expert = (lane // PAD).astype(jnp.float32)
    lane_slot = (lane % PAD).astype(jnp.float32)
    earlier = (
        lax.broadcasted_iota(jnp.int32, (rows, rows), 1)
        < lax.broadcasted_iota(jnp.int32, (rows, rows), 0)
    ).astype(jnp.float32).astype(jnp.bfloat16)
    for s in range(steps):
        r0, r1 = rgb[s, :, 0:1], rgb[s, :, 1:2]
        g0, g1 = rgb[s, :, 2:3], rgb[s, :, 3:4]
        first = jnp.where(r0 == lane_expert, 1.0, 0.0)
        second = jnp.where(r1 == lane_expert, 1.0, 0.0)
        routed = first + second
        before = jnp.dot(earlier, routed.astype(jnp.bfloat16), preferred_element_type=jnp.float32)
        here = jnp.where(before == lane_slot, 1.0, 0.0)
        sel = routed * here
        pmat[s] = sel.T.astype(jnp.bfloat16)
        weight = STEP_SIZE * (g0 * first + g1 * second) * here
        high = weight.astype(jnp.bfloat16)
        cmat[s, 0:rows, :] = high
        cmat[s, rows:, :] = (weight - high.astype(jnp.float32)).astype(jnp.bfloat16)

    def a_copy(c, k):
        d = peer(k)
        return remote(
            send_a.at[slab(d), cols(c)], recv_a.at[slab(me), cols(c)],
            a_ssem.at[c, k - 1], a_rsem.at[c, k - 1], "expert", d,
        )

    def b_copy(c, k):
        d = peer(k)
        return remote(
            send_b.at[slab(d), cols(c)], recv_b.at[slab(me), cols(c)],
            b_ssem.at[c, k - 1], b_rsem.at[c, k - 1], "expert", d,
        )

    def s_copy(s, k):
        d = peer(k)
        return remote(
            send_s.at[s, slab(d)], recv_s.at[s, slab(me)],
            s_ssem.at[s, k - 1], s_rsem.at[s, k - 1], "expert", d,
        )

    own = pl.ds(pl.multiple_of(me * PAD, PAD), PAD)

    def pack_a(step, c):
        packed = jnp.dot(
            pmat[step], adj[:, cols(c)].astype(jnp.bfloat16), preferred_element_type=jnp.float32
        ).astype(jnp.bfloat16)
        send_a[:, cols(c)] = packed
        for k in range(1, experts):
            a_copy(c, k).start()
        recv_a[own, cols(c)] = send_a[own, cols(c)]

    def pack_s(s):
        for c in range(CHUNKS):
            send_s[s, :, cols(c)] = jnp.dot(
                pmat[s], sts[s, :, cols(c)], preferred_element_type=jnp.float32
            ).astype(jnp.bfloat16)
        for k in range(1, experts):
            s_copy(s, k).start()
        recv_s[s, own, :] = send_s[s, own, :]

    own_states.wait()
    for k in range(1, steps):
        st_copy(k).wait()
    pack_s(steps - 1)
    own_terminal.wait()
    for c in range(CHUNKS):
        pack_a(steps - 1, c)

    for copy in weights[:CHUNKS]:
        copy.wait()

    def make_slopes(s):
        for k in range(1, experts):
            s_copy(s, k).wait()
        rows_in = recv_s[s]
        for c in range(CHUNKS):
            part = pl.ds(c * fc, fc)
            pre = jnp.dot(rows_in, win[:, part], preferred_element_type=jnp.float32)
            slopes[:, part] = gelu_slope(pre)

    make_slopes(steps - 1)
    for copy in weights[CHUNKS:]:
        copy.wait()

    nt = (((1,), (1,)), ((), ()))

    def out_remote(s):
        return remote(
            collect.at[s], out.at[0, block_rows(t)], o_ssem.at[s], o_rsem.at[t], "tm", s
        )

    def out_local(s):
        return pltpu.make_async_copy(collect.at[s], out.at[0, block_rows(t)], loc_sem.at[3])

    def one_round(turn, carry):
        s = steps - 1 - turn
        more = turn < steps - 1

        @pl.when(more)
        def _():
            pack_s(s - 1)

        for c in range(CHUNKS):
            for k in range(1, experts):
                a_copy(c, k).wait()
            term = lax.dot_general(
                recv_a[:, cols(c)], wout[:, cols(c)], nt, preferred_element_type=jnp.float32
            )
            if c == 0:
                back[...] = term
            elif c < CHUNKS - 1:
                back[...] += term
            else:
                hidden[...] = ((back[...] + term) * slopes[...]).astype(jnp.bfloat16)
        for c in range(CHUNKS):
            send_b[:, cols(c)] = lax.dot_general(
                hidden[...], win[cols(c), :], nt, preferred_element_type=jnp.float32
            ).astype(jnp.bfloat16)
            for k in range(1, experts):
                b_copy(c, k).start()
            recv_b[own, cols(c)] = send_b[own, cols(c)]

        @pl.when(more)
        def _():
            make_slopes(s - 1)

        for c in range(CHUNKS):
            for k in range(1, experts):
                b_copy(c, k).wait()
            both = jnp.dot(cmat[s], recv_b[:, cols(c)], preferred_element_type=jnp.float32)
            adj[:, cols(c)] = adj[:, cols(c)] + (both[0:rows] + both[rows:])
            collect[s, :, cols(c)] = adj[:, cols(c)]

            @pl.when(more)
            def _():
                pack_a(s - 1, c)

        @pl.when(s == t)
        def _():
            out_local(s).start()

        @pl.when(s != t)
        def _():
            out_remote(s).start()

        return carry

    lax.fori_loop(0, steps, one_round, 0)

    out_local(t).wait()
    for k in range(1, steps):
        out_remote(tm_peer(k)).wait_send()
    for k in range(1, steps):
        b = tm_peer(k)
        remote(collect.at[b], out.at[0, block_rows(b)], o_ssem.at[b], o_rsem.at[b], "tm", b).wait_recv()


def per_device(states, terminal, gates, routes, w_in, w_out):
    steps = lax.axis_size("tm")
    experts = lax.axis_size("expert")
    width = states.shape[2]
    ff = w_in.shape[2]
    top = routes.shape[2]
    tokens = states.shape[1]
    rows = tokens // steps
    cap = min(rows, (3 * MB * top + 2 * experts - 1) // (2 * experts))
    slots = experts * PAD
    rg = jnp.concatenate([routes[0].astype(jnp.float32), gates[0]], axis=1)
    rg = jnp.pad(rg, ((0, 0), (0, 128 - 2 * top)))
    dma = pltpu.SemaphoreType.DMA
    bf = jnp.bfloat16
    return pl.pallas_call(
        functools.partial(kernel, steps, experts, cap, rows),
        out_shape=jax.ShapeDtypeStruct(states.shape, jnp.float32),
        in_specs=[pl.BlockSpec(memory_space=pl.ANY)] * 5,
        out_specs=pl.BlockSpec(memory_space=pl.ANY),
        scratch_shapes=[
            pltpu.VMEM((width, ff), bf),
            pltpu.VMEM((ff, width), bf),
            pltpu.VMEM((rows, width), jnp.float32),
            pltpu.VMEM((steps, rows, width), bf),
            pltpu.VMEM((steps, rows, 128), jnp.float32),
            pltpu.VMEM((steps, slots, rows), bf),
            pltpu.VMEM((steps, 2 * rows, slots), bf),
            pltpu.VMEM((steps, slots, width), bf),
            pltpu.VMEM((steps, slots, width), bf),
            pltpu.VMEM((slots, width), bf),
            pltpu.VMEM((slots, width), bf),
            pltpu.VMEM((slots, width), bf),
            pltpu.VMEM((slots, width), bf),
            pltpu.VMEM((slots, ff), jnp.float32),
            pltpu.VMEM((slots, ff), jnp.float32),
            pltpu.VMEM((slots, ff), bf),
            pltpu.VMEM((steps, rows, width), jnp.float32),
            dma((2, CHUNKS)),
            dma((4,)),
            dma((steps - 1,)),
            dma((steps - 1,)),
            dma((steps - 1,)),
            dma((steps - 1,)),
            dma((steps, experts - 1)),
            dma((steps, experts - 1)),
            dma((CHUNKS, experts - 1)),
            dma((CHUNKS, experts - 1)),
            dma((CHUNKS, experts - 1)),
            dma((CHUNKS, experts - 1)),
            dma((steps,)),
            dma((steps,)),
        ],
        compiler_params=pltpu.CompilerParams(
            collective_id=0, has_side_effects=True, vmem_limit_bytes=60 * 1024 * 1024
        ),
    )(states, terminal, rg, w_in, w_out)


def solution(mesh):
    placed = (
        P("tm", "expert", None),
        P("expert", None),
        P("tm", "expert", None),
        P("tm", "expert", None),
        P("expert", None, None),
        P("expert", None, None),
    )
    return jax.shard_map(
        per_device, mesh=mesh, in_specs=placed, out_specs=P("tm", "expert", None), check_vma=False
    )
```

time: 343 us -> 167 us (0.49)
  Pallas kernels: 0 us -> 162 us
  blocking collectives: 103 us -> 0 us
  waiting for transfers between devices: 93.2 us -> 0 us
  matrix products: 63.9 us -> 0 us
  starting transfers between devices: 36.8 us -> 0 us
  local copies, waits for them, and re-layouts: 27.7 us -> 3.05 us
  other arithmetic: 16.1 us -> 1.37 us
    pallas_call x0 -> x1, Pallas kernels: none -> 162 us  [per_device(): pl.pallas_call(functools.partial(kernel, steps, experts, cap, rows), out_...]
    all_to_all x5 -> x0, blocking collectives: 93.3 us -> none  [the longest x4 75.4 us: one_round(): lax.all_to_all(state_send, 'expert', split_axis=1, concat_axis=1, tiled=T...]
    all_to_all x10 -> x0, waiting for transfers between devices: 93.2 us -> none  [the longest x4 55.9 us: one_round(): lax.all_to_all(answers, 'expert', split_axis=1, concat_axis=1, tiled=True)]
    dot_general x8 -> x0, matrix products: 63.9 us -> none  [the longest x4 44.5 us: backprop(): lax.dot_general(hidden, weight_in, (((1,), (1,)), ((), ())), preferred_el...]
    all_to_all x10 -> x0, starting transfers between devices: 36.8 us -> none  [the longest x4 14.5 us: one_round(): lax.all_to_all(adjoint_send, 'expert', split_axis=1, concat_axis=1, tiled...]
    gather x20 -> x0, local copies, waits for them, and re-layouts: 10.4 us -> none  [the longest x16 7.41 us: pack(): rows[source_row]]
    all_gather x1 -> x0, blocking collectives: 9.65 us -> none  [per_device(): every_route = lax.all_gather(routes, 'tm', axis=0, tiled=True)]
    reshape x24 -> x0, local copies, waits for them, and re-layouts: 5.35 us -> none  [the longest x4 3.51 us: vjp_rows(): backprop(adjoint_rows, gelu_slope(preact)).reshape(adjoint_rows.shape)]
  transfers between devices with their start and end apart: 10 -> 0, of which waited for: 8 -> 0; matrix products, arithmetic and copies ran while one was open for 8% -> 0% of each run, Pallas kernels for 0% -> 0%
where the time goes in v1:
time: 167 us
  Pallas kernels  162 us (97%)
  local copies, waits for them, and re-layouts  3.05 us (2%)
    pallas_call x1, Pallas kernels, per_device(): pl.pallas_call(functools.partial(kernel, steps, experts, cap, rows), out_...  162 us

profile of v1, /device:TPU:0, one launch (start us, length us, event | category | flops | bytes accessed | tf_op | source)
XLA Modules:
  0.0 166.6 jit_solution(8720736985635679013)
XLA Ops:
  0.0 0.7 convert_bitcast_fusion
  0.7 0.7 pad_maximum_fusion
  1.4 0.1 copy.9
  1.5 0.6 pad.4.rg
  2.1 162.1 %shard_map.64 = f32[1,128,2048]{2,1,0:T(8,128)} custom-call(bf16[1,128,2048]{2,1,0:T(8,128)(2,1)} %states.1, f32[128,2048]{1,0:T(8,128)} %terminal.1, f32[128,128]{1,0:T(8,128)} %pad.4.rg, bf16[1,2048,2048]{2,1,0:T(8,128)(2,1)} %w_in.1, bf16[1,2048,2048]{2,1,0:T(8,128)(2,1)} %w_out.1), custom_call_target="tpu_custom_call" | custom-call | tf_op jit(solution)/shard_map/pallas_call | solution.py:293
  164.3 2.3 %copy.11 = f32[1,128,2048]{2,1,0:T(8,128)} copy(f32[1,128,2048]{2,1,0:T(8,128)} %shard_map.64) | data formatting | bytes 2097152
